TPU v7x, 256 devices: a whole 4x4x8 slice. The times are simulated.
256 devices in a mesh: area: 16 (over x, y), sec: 16 (over z, core).
Axes of the slice: x: 4, y: 4, z: 8, core: 2. Of those that a mesh axis runs over, the one named last changes fastest.
Arguments:
- spikes: int32 [16, 3, 16384], P('area', None, 'sec'), may hold values 0 or 1
- intra_weight: float32 [16, 128, 8, 128, 128], P('area', 'sec'), may hold values from -0.5 to 0.5
- intra_dest: int32 [16, 128, 8], P('area'), may hold values from 0 to 127, all different within a row
- inter_weight: float32 [16, 128, 2, 128, 128], P('area', 'sec'), may hold values from -0.5 to 0.5
- inter_target: int32 [16, 16, 2], P(None, 'sec'), may hold values from 0 to 15, all different within a row
- v_init: float32 [16, 16384], P('area', 'sec'), may hold values from 0 to 1
- leak: float32 [16, 16384], P('area', 'sec'), may hold values from 0.3 to 0.95
Outputs:
- potential: float32 [16, 16384], P('area', 'sec')
Inputs may be any that keep to these rules, and one draw needn't show every extreme that they name: `intra_dest`: the 8 target blocks of a source block are distinct; some blocks receive far more synapse blocks than others. `inter_target`: the 2 target areas of a section are distinct; some areas are targeted far more often than others.
All inputs are finite; a program needn't handle non-finite values. No bound on the sum of `spikes` on one device may be relied on, other than what follows from the above.
Results may differ from a plain program's by a relative error of at most 0.000058.
Values sent between devices are 32-bit elements; how exact they have to be, the bound alone decides.
A program may use at most 64 MiB of HBM per device.

v0:
```python
import jax
import jax.numpy as jnp
from jax import lax
from jax.sharding import PartitionSpec as P


def body(spikes, intra_weight, intra_dest, inter_weight, inter_target, v_init, leak):
    blocks = intra_weight.shape[1]
    width = intra_weight.shape[-1]
    steps = spikes.shape[1]
    columns = steps * width
    later = (steps - 1) * width
    section = lax.axis_index("sec")
    area_here = lax.axis_index("area")
    block_count = intra_dest.shape[1]
    spiking = spikes[0].astype(jnp.float32).reshape(steps, blocks, width)
    previous = spiking[:-1]
    intra_part = jnp.einsum(
        "tkn,kfnm->kftm", spiking, intra_weight[0], precision=lax.Precision.HIGHEST
    )
    fanout = intra_part.shape[1]
    intra_rows = intra_part.reshape(blocks * fanout, columns)
    dest_flat = intra_dest[0].reshape(-1)
    my_dest = lax.dynamic_slice_in_dim(dest_flat, section * blocks * fanout, blocks * fanout, 0)
    picker = (jnp.arange(block_count, dtype=jnp.int32)[:, None] == my_dest[None, :]).astype(
        jnp.float32
    )
    block_grid = jnp.dot(
        picker, intra_rows, precision=lax.Precision.HIGHEST, preferred_element_type=jnp.float32
    )
    intra_current = lax.psum_scatter(block_grid, "sec", scatter_dimension=0, tiled=True)
    inter_part = jnp.einsum(
        "tkn,kjnm->kjtm", previous, inter_weight[0], precision=lax.Precision.HIGHEST
    )
    targets_all = inter_target[:, 0, :]
    fan_areas = targets_all.shape[1]
    picker = (targets_all == area_here).astype(jnp.float32)
    inter_current = jnp.einsum(
        "aj,akjx->kx",
        picker,
        lax.all_gather(inter_part.reshape(1, blocks, fan_areas, later), "area", axis=0, tiled=True),
        precision=lax.Precision.HIGHEST,
    )
    inter_full = jnp.concatenate([jnp.zeros((blocks, width), jnp.float32), inter_current], axis=1)
    current = (intra_current + inter_full).reshape(blocks, steps, width)
    current = current.transpose(1, 0, 2).reshape(steps, blocks * width)
    drive = spikes[0].astype(jnp.float32)
    potential = v_init[0]
    decay = leak[0]
    for moment in range(steps):
        potential = decay * potential * (1.0 - drive[moment]) + current[moment]
    return potential[None]


def solution(mesh):
    in_specs = (
        P("area", None, "sec"),
        P("area", "sec", None, None, None),
        P("area", None, None),
        P("area", "sec", None, None, None),
        P(None, "sec", None),
        P("area", "sec"),
        P("area", "sec"),
    )
    out_specs = P("area", "sec")
    return jax.shard_map(body, mesh=mesh, in_specs=in_specs, out_specs=out_specs, check_vma=False)
```

profile of v0, /device:TPU:1, one launch (start us, length us, event | category | flops | bytes accessed | tf_op | source)
XLA Modules:
  0.0 130.5 jit_solution(11523697200835841770)
XLA Ops:
  6.5 0.0 copy-start
  6.5 0.0 copy-start.4
  6.5 0.0 copy-start.3
  6.5 0.0 copy-start.2
  6.5 0.0 all-reduce.4.cloned.1.call-start
  6.6 0.9 copy.12
  7.5 0.1 reshape_squeeze.3
  7.6 0.7 convert_element_type.11
  8.3 0.1 dynamic_slice.3
  8.4 4.4 %fusion.2 = f32[8,8,3,128]{3,2,1,0:T(4,128)S(1)} fusion(f32[1,8,8,128,128]{4,3,2,1,0:T(8,128)} %param.8, f32[3,8,128,1]{2,1,0,3:T(8,128)S(1)} %bitcast.60), kind=kOutput, calls=%fused_computation.2 | convolution fusion | flops 37748736 | bytes 4304896 | tf_op jit(solution)/shard_map/tkn,kfnm->kftm/dot_general | solution.py:18
  12.8 0.9 fusion.8
  13.7 0.0 all-reduce.4.cloned.1.call-update
  13.8 0.0 copy-done
  13.8 0.7 convolution_bitcast_fusion
  14.5 19.9 %all_gather.3 = f32[16,8,2,256]{3,1,2,0:T(8,128)S(1)} all-gather(f32[1,8,2,256]{3,1,2,0:T(8,128)S(1)} %copy.15), channel_id=1, replica_groups=mesh['area'=16,'sec'=16] {'area'}, dimensions={0}, use_global_device_ids=true | all-gather | bytes 278528 | tf_op jit(solution)/shard_map/all_gather | solution.py:41
  34.4 0.0 copy-done.3
  34.4 0.3 fusion.6
  34.8 0.0 copy-done.4
  34.8 0.6 dynamic-slice
  36.1 86.3 %all-reduce.4.cloned.1.call-done = f32[128,384]{1,0:T(8,128)} async-done(((f32[128,384]{1,0:T(8,128)}), f32[128,384]{1,0:T(8,128)}) %all-reduce.4.cloned.1.call-update) | async-done | bytes 196624
  122.3 0.7 fusion.13
  123.0 0.0 copy-done.2
  123.0 0.0 copy-done.1
  123.0 0.6 fusion.17
  (7 shorter events, 0.0 us)
Async XLA Ops:
  6.5 7.2 %copy-start = (f32[1,8,2,128,128]{4,3,2,1,0:T(8,128)S(1)}, f32[1,8,2,128,128]{4,3,2,1,0:T(8,128)}, u32[]{:S(2)}) copy-start(f32[1,8,2,128,128]{4,3,2,1,0:T(8,128)} %param.10) | copy-start | bytes 3145732
  6.5 28.3 %copy-start.4 = (u32[256]{0:T(256)S(1)}, u32[256]{0:T(256)}, u32[]{:S(2)}) copy-start(u32[256]{0:T(256)} %constant.29) | copy-start | bytes 3076
  6.5 27.9 %copy-start.3 = (s32[16,1,2]{0,2,1:T(2,128)S(1)}, s32[16,1,2]{0,2,1:T(2,128)}, u32[]{:S(2)}) copy-start(s32[16,1,2]{0,2,1:T(2,128)} %param.11) | copy-start | bytes 388
  6.5 116.5 %copy-start.2 = (f32[1,1024]{1,0:T(1,128)S(1)}, f32[1,1024]{1,0:T(1,128)}, u32[]{:S(2)}) copy-start(f32[1,1024]{1,0:T(1,128)} %param.12) | copy-start | bytes 12292
  6.5 116.5 %copy-start.1 = (f32[1,1024]{1,0:T(1,128)S(1)}, f32[1,1024]{1,0:T(1,128)}, u32[]{:S(2)}) copy-start(f32[1,1024]{1,0:T(1,128)} %param.13) | copy-start | bytes 12292
  6.5 115.8 %all-reduce.4.cloned.1.call-start = ((), (), s32[]{:S(2)}) async-start(), calls=%async_computation | async-start | bytes 393216
Sparse Core Ops, SparseCore 0:
  13.9 108.4 all-reduce.3
where the time goes:
time: 131 us
  waiting for transfers between devices  86.3 us (66%)
  blocking collectives  19.9 us (15%)
  between operations  14.2 us (11%)
  matrix products  6.37 us (5%)
  other arithmetic  2.05 us (2%)
  local copies, waits for them, and re-layouts  1.68 us (1%)
    unnamed x2, waiting for transfers between devices  86.3 us
    all_gather x1, blocking collectives, body(): lax.all_gather(inter_part.reshape(1, blocks, fan_areas, later), 'area', a...  19.9 us
    dot_general x1, matrix products, body(): jnp.einsum('tkn,kfnm->kftm', spiking, intra_weight[0], precision=lax.Prec...  4.44 us
  transfers between devices with their start and end apart: 1, of which 1 were waited for; matrix products, arithmetic and copies ran while one was open for 1% of the time, Pallas kernels for 0%

commit v1 on v0

--- a/solution.py
+++ b/solution.py
@@ -38,7 +38,17 @@
     inter_current = jnp.einsum(
         "aj,akjx->kx",
         picker,
-        lax.all_gather(inter_part.reshape(1, blocks, fan_areas, later), "area", axis=0, tiled=True),
+        jnp.concatenate(
+            lax.all_to_all(
+                jnp.stack(
+                    [inter_part.reshape(1, blocks, fan_areas, later)] * lax.axis_size("area")
+                ),
+                "area",
+                0,
+                0,
+            ),
+            axis=0,
+        ),
         precision=lax.Precision.HIGHEST,
     )
     inter_full = jnp.concatenate([jnp.zeros((blocks, width), jnp.float32), inter_current], axis=1)

time: 131 us -> 140 us (1.069)
  waiting for transfers between devices: 86.3 us -> 107 us
  blocking collectives: 19.9 us -> 0 us
  starting transfers between devices: 0.04 us -> 7.63 us
    unnamed x2, waiting for transfers between devices: 86.3 us -> 107 us
    all_gather x1 -> x0, blocking collectives: 19.9 us -> none  [body(): lax.all_gather(inter_part.reshape(1, blocks, fan_areas, later), 'area', a...]
    all_to_all x0 -> x1, starting transfers between devices: none -> 7.58 us  [body(): lax.all_to_all(jnp.stack([inter_part.reshape(1, blocks, fan_areas, later)...]
  transfers between devices with their start and end apart: 1 -> 2, of which waited for: 1 -> 1; matrix products, arithmetic and copies ran while one was open for 1% -> 5% of each run, Pallas kernels for 0% -> 0%
where the time goes in v1:
time: 140 us
  waiting for transfers between devices  107 us (76%)
  between operations  14.1 us (10%)
  starting transfers between devices  7.63 us (5%)
  matrix products  6.35 us (5%)
  local copies, waits for them, and re-layouts  2.8 us (2%)
  other arithmetic  2.14 us (2%)
    unnamed x2, waiting for transfers between devices  107 us
    all_to_all x1, starting transfers between devices, body(): lax.all_to_all(jnp.stack([inter_part.reshape(1, blocks, fan_areas, later)...  7.58 us
    dot_general x1, matrix products, body(): jnp.einsum('tkn,kfnm->kftm', spiking, intra_weight[0], precision=lax.Prec...  4.44 us
  transfers between devices with their start and end apart: 2, of which 1 were waited for; matrix products, arithmetic and copies ran while one was open for 5% of the time, Pallas kernels for 0%

profile of v1, /device:TPU:1, one launch (start us, length us, event | category | flops | bytes accessed | tf_op | source)
XLA Modules:
  0.0 139.6 jit_solution(8487511697358232650)
XLA Ops:
  6.5 0.0 copy-start
  6.5 0.0 copy-start.4
  6.5 0.8 convert_element_type.11
  7.4 0.4 copy-done
  7.8 0.7 convolution_bitcast_fusion
  8.5 0.8 stack.3
  9.3 7.6 %all-to-all-start = ((f32[16,1,8,2,256]{4,3,2,1,0:T(2,128)}), f32[16,1,8,2,256]{4,3,2,1,0:T(2,128)S(1)}, u32[]{:S(2)}, u32[]{:S(2)}) async-start(f32[16,1,8,2,256]{4,3,2,1,0:T(2,128)} %stack.3), calls=%async_computation | async-start | bytes 524288 | tf_op jit(solution)/shard_map/all_to_all | solution.py:42
  16.9 0.0 all-reduce.4.cloned.1.call-start
  16.9 0.8 copy.12
  17.7 0.1 reshape_squeeze.3
  17.8 0.1 dynamic_slice.3
  17.9 4.4 %fusion.2 = f32[8,8,3,128]{3,2,1,0:T(4,128)S(1)} fusion(f32[1,8,8,128,128]{4,3,2,1,0:T(8,128)} %param.8, f32[3,8,128,1]{2,1,0,3:T(8,128)S(1)} %bitcast.62), kind=kOutput, calls=%fused_computation.2 | convolution fusion | flops 37748736 | bytes 4304896 | tf_op jit(solution)/shard_map/tkn,kfnm->kftm/dot_general | solution.py:18
  22.3 0.9 fusion.8
  23.2 0.0 all-reduce.4.cloned.1.call-update
  23.3 0.0 copy-done.4
  23.3 0.6 dynamic-slice
  24.5 0.0 copy-done.3
  24.5 0.0 all-to-all-done
  24.5 0.3 fusion.6
  24.9 106.5 %all-reduce.4.cloned.1.call-done = f32[128,384]{1,0:T(8,128)} async-done(((f32[128,384]{1,0:T(8,128)}), f32[128,384]{1,0:T(8,128)}) %all-reduce.4.cloned.1.call-update) | async-done | bytes 196624
  131.4 0.7 fusion.13
  132.1 0.0 copy-done.2
  132.1 0.0 copy-done.1
  132.1 0.6 fusion.17
  (8 shorter events, 0.0 us)
Async XLA Ops:
  6.5 1.2 copy-start
  6.5 16.7 %copy-start.4 = (u32[256]{0:T(256)S(1)}, u32[256]{0:T(256)}, u32[]{:S(2)}) copy-start(u32[256]{0:T(256)} %constant.29) | copy-start | bytes 3076
  6.5 18.0 %copy-start.3 = (s32[16,1,2]{0,2,1:T(2,128)S(1)}, s32[16,1,2]{0,2,1:T(2,128)}, u32[]{:S(2)}) copy-start(s32[16,1,2]{0,2,1:T(2,128)} %param.11) | copy-start | bytes 388
  6.5 125.6 %copy-start.2 = (f32[1,1024]{1,0:T(1,128)S(1)}, f32[1,1024]{1,0:T(1,128)}, u32[]{:S(2)}) copy-start(f32[1,1024]{1,0:T(1,128)} %param.12) | copy-start | bytes 12292
  6.5 125.6 %copy-start.1 = (f32[1,1024]{1,0:T(1,128)S(1)}, f32[1,1024]{1,0:T(1,128)}, u32[]{:S(2)}) copy-start(f32[1,1024]{1,0:T(1,128)} %param.13) | copy-start | bytes 12292
  9.3 15.3 %all-to-all-start = ((f32[16,1,8,2,256]{4,3,2,1,0:T(2,128)}), f32[16,1,8,2,256]{4,3,2,1,0:T(2,128)S(1)}, u32[]{:S(2)}, u32[]{:S(2)}) async-start(f32[16,1,8,2,256]{4,3,2,1,0:T(2,128)} %stack.3), calls=%async_computation | async-start | bytes 524288 | tf_op jit(solution)/shard_map/all_to_all | solution.py:42
  16.9 114.6 %all-reduce.4.cloned.1.call-start = ((), (), s32[]{:S(2)}) async-start(), calls=%async_computation.1 | async-start | bytes 393216
Sparse Core Ops, SparseCore 0:
  23.4 108.0 all-reduce.3
